TPU v7x, 256 devices: a whole 4x4x8 slice. The times are simulated.
256 devices in a mesh: gz: 4 (over z_lo, core), xy: 64 (over y, x, z_hi).
Axes of the slice: x: 4, y: 4, z: 8 (z_hi: 4, z_lo: 2; z = z_hi * 2 + z_lo), core: 2. Of those that a mesh axis runs over, the one named last changes fastest.
Arguments:
- features: float32 [64, 128, 28, 256], P('gz', 'xy'), may hold values from -6 to 6
- block_mask: int32 [32, 64, 14], P('gz', 'xy'), may hold values 0 or 1
- near_kernel_weight: float32 [27, 256, 256], P(None, None, 'xy'), may hold values from -0.078125 to 0.078125
- far_kernel_weight: float32 [27, 256, 256], P(None, None, 'xy'), may hold values from -0.078125 to 0.078125
Outputs:
- section_out: float32 [64, 128, 28, 256], P('gz', 'xy')
All inputs are finite; a program needn't handle non-finite values. No bound on the sum of `block_mask` on one device may be relied on, other than what follows from the above.
Results may differ from a plain program's by a relative error of at most 0.00005.
Values sent between devices are 32-bit elements; how exact they have to be, the bound alone decides.
No kernel may reach another device: no remote copies, remote signals or barrier semaphores. Data moves between devices by JAX's collectives and lax.ppermute only.
A program may use at most 128 MiB of HBM per device.

v0:
```python
import jax
import jax.numpy as jnp
from jax import lax
from jax.experimental import pallas as pl
from jax.experimental.pallas import tpu as pltpu
from jax.sharding import Mesh, PartitionSpec as P


B = 2
F32, BF16 = jnp.float32, jnp.bfloat16
AXES = ("zl", "core", "y", "xh", "xl", "zh")
GROUP = ("zl", "core", "y", "xh")
PLANE = 28 * 8
EARLY = 14
HALVES = [(d, start) for d in (0, 1, 3, 2) for start in (0, 2)]
WHOLES = [(0, 0), (1, 0), (3, 0), (2, 0)]


def split(value):
    high = value.astype(BF16)
    return high, (value - high.astype(F32)).astype(BF16)


def triple(value):
    high, low = split(value)
    return jnp.concatenate([high, low, high], 1)


def tap_matrix(buf, core, slot):
    tiles = buf[core, :, :, :, slot].reshape(32, 2, 8, 128)
    even, odd = tiles[:, 0], tiles[:, 1]
    top = lax.broadcasted_iota(jnp.int32, (32, 8, 128), 1) < 4
    left = jnp.where(top, even, pltpu.roll(odd, 4, 1)).reshape(256, 128)
    right = jnp.where(top, pltpu.roll(even, 4, 1), odd).reshape(256, 128)
    left_high, left_low = split(left)
    right_high, right_low = split(right)
    return jnp.concatenate([left_high, right_high, left_high, right_high, left_low, right_low], 1)


def fetch(spot, pieces, table, buf, sem):
    copies = []
    for n, piece in enumerate(pieces):
        core = spot[0] if n < len(table) else 1 - spot[0]
        d, start = table[n % len(table)]
        place = (jnp.where(core == 0, spot[1], spot[2]) - d) & 3
        for e in range(piece.shape[0]):
            first, second = jnp.where(core == 0, start + e, place), jnp.where(core == 0, place, start + e)
            copies.append(pltpu.make_async_copy(piece.at[e], buf.at[core, first, second], sem.at[len(copies)]))
            copies[-1].start()
    return copies


def dot(a, b):
    return lax.dot_general(a, b, (((1,), (1,)), ((), ())), preferred_element_type=F32)


def weave(value, reach):
    row = lax.broadcasted_iota(jnp.int32, value.shape, 0) & 7
    below = jnp.where(row < reach, 0.0, pltpu.roll(value, reach, 0))
    above = jnp.where(row >= 8 - reach, 0.0, pltpu.roll(value, value.shape[0] - reach, 0))
    return below, value, above


def add(acc, source, b, step, weight, taken=(0, 28), given=(0, 28)):
    planes = range(max(0, -step), min(4, 4 - step))
    if taken[1] - taken[0] == 28:
        runs = [(planes[0], len(planes))]
    else:
        runs = [(g, 1) for g in planes]
    size = (taken[1] - taken[0]) * 8
    left = [source[b, pl.ds((g + step) * PLANE + taken[0] * 8, size + (n - 1) * PLANE)] for g, n in runs]
    product = dot(left[0] if len(left) == 1 else jnp.concatenate(left, 0), weight)
    for i, (g, n) in enumerate(runs):
        start, count = g * PLANE + given[0] * 8, size + (n - 1) * PLANE
        for half in range(2):
            acc[half, start : start + count] += product[i * count : (i + 1) * count, half * 128 : half * 128 + 128]


def prepare(x_ref, xn, mask):
    lane = lax.broadcasted_iota(jnp.int32, (PLANE, 128), 1)
    row = lax.broadcasted_iota(jnp.int32, (PLANE, 128), 0) >> 3

    @pl.loop(0, 4)
    def _(g):
        cells = pl.ds(g * 8, 8)
        for y in range(0, 32, 8):
            block = jnp.swapaxes(x_ref[cells, y : y + 8], 0, 1)
            for i in range(0, min(8, 28 - y), 2):
                cell = block[i : i + 2].reshape(16, 256)
                for b, value in enumerate(weave(cell, 1)):
                    xn[b, pl.ds(pl.multiple_of(g * PLANE + (y + i) * 8, 16), 16)] = triple(value)
            if y == 24:
                flags = jnp.concatenate([block[4, :, :128]] * 28, 0)
        active = jnp.sum(jnp.where(row == lane, flags, 0.0), 1, keepdims=True)
        mask[pl.ds(pl.multiple_of(g * PLANE, 16), PLANE)] = jnp.broadcast_to(active, (PLANE, 128))


def near_body(spot, x_ref, *refs):
    pieces, (hidden, middle, buf, xn, acc, mask, sem) = refs[:16], refs[16:]
    copies = fetch(spot, pieces, HALVES, buf, sem)
    prepare(x_ref, xn, mask)
    acc[...] = jnp.zeros_like(acc)
    for copy in copies:
        copy.wait()

    def weight(tap):
        core = jnp.where(tap < EARLY, 0, 1)
        return tap_matrix(buf, core, tap - EARLY * core)

    for a in range(3):

        @pl.loop(0, 3)
        def _(b):
            tap = a * 9 + b * 3
            add(acc, xn, b, a - 1, weight(tap + 1))
            add(acc, xn, b, a - 1, weight(tap), (0, 12), (16, 28))
            add(acc, xn, b, a - 1, weight(tap + 2), (16, 28), (0, 12))

    middle[...] = tap_matrix(buf, 1, EARLY - 1)
    for half in range(2):
        hidden[half] = mask[...] * jnp.maximum(acc[half], 0.0)


def far_body(spot, hidden, middle, *refs):
    pieces, (o_ref, buf, xf, acc, sem) = refs[:8], refs[8:]
    copies = fetch(spot, pieces, WHOLES, buf, sem)

    @pl.loop(0, 56)
    def _(n):
        rows = pl.ds(pl.multiple_of(n * 16, 16), 16)
        cell = jnp.concatenate([hidden[half, rows] for half in range(2)], 1)
        for b, value in enumerate(weave(cell, 2)):
            xf[b, rows] = triple(value)

    acc[...] = jnp.zeros_like(acc)
    add(acc, xf, 1, 0, middle[...])
    for copy in copies:
        copy.wait()

    for b in (0, 2):
        add(acc, xf, b, 0, tap_matrix(buf, b // 2, 3 - b // 2 * 3))
    for b in range(3):
        for core, a in ((0, 0), (1, 2)):
            add(acc, xf, b, 2 * (a - 1), tap_matrix(buf, core, b + core))

    @pl.loop(0, 4)
    def _(g):
        for k in range(8):
            for half in range(2):
                o_ref[g * 8 + k, :28, half * 128 : half * 128 + 128] = acc[half, pl.ds(g * PLANE + k, 28, stride=8)]


def call(body, blocks, pieces, outs, scratch, flops):
    vmem = pl.BlockSpec(memory_space=pltpu.VMEM)
    taps = pieces[0].shape[2]
    return pl.pallas_call(
        body,
        out_shape=[jax.ShapeDtypeStruct(shape, dtype) for shape, dtype in outs],
        in_specs=[pl.BlockSpec(memory_space=pltpu.SMEM)]
        + [vmem] * (len(blocks) - 1)
        + [pl.BlockSpec(memory_space=pl.ANY)] * len(pieces),
        out_specs=[vmem] * len(outs),
        scratch_shapes=[pltpu.VMEM((2, 4, 4, 4, taps, 8, 128), F32)]
        + [pltpu.VMEM(shape, dtype) for shape, dtype in scratch]
        + [pltpu.SemaphoreType.DMA((32,))],
        compiler_params=pltpu.CompilerParams(vmem_limit_bytes=60 << 20),
        cost_estimate=pl.CostEstimate(flops=flops, bytes_accessed=8_000_000, transcendentals=0),
    )(*blocks, *pieces)


def send(value, axis, pairs):
    return lax.ppermute(value, axis, pairs)


def shift(value, axis, d):
    pairs = []
    for n in range(32):
        core, y, x = n // 16, n // 4 % 4, n % 4
        if (axis == "y") == (core == 0):
            y = (y + d) % 4
        else:
            x = (x + d) % 4
        pairs.append((n, core * 16 + y * 4 + x))
    return send(value, ("core", "y", "xh", "xl"), pairs)


def in_order(parts, which):
    return jnp.stack([lax.select_n(which[j], *parts) for j in range(4)], 0)


def tiles(weight):
    taps = weight.shape[0]
    return weight.transpose(0, 2, 1).reshape(taps, 4, 2, 128).transpose(0, 2, 1, 3).reshape(taps, 8, 128)


def along_z(mine):
    zl, zh = lax.axis_index("zl"), lax.axis_index("zh")

    def pairs(distance):
        route = [(z, (z + (distance if z % 2 == 0 else -distance)) % 8) for z in range(8)]
        return [((s % 2) * 4 + s // 2, (t % 2) * 4 + t // 2) for s, t in route]

    near, following, far = [send(mine, ("zl", "zh"), pairs(-d)) for d in (1, 2, 3)]
    which = []
    for j in range(4):
        ahead = (j - zh) % 4
        which.append(jnp.where(ahead == 0, 0, jnp.where(ahead == 2, 3, jnp.where((ahead == 1) == (zl == 1), 1, 2))))
    return in_order([mine, near, following, far], which)


def gather(near_weight, far_weight, payload):
    core, y = lax.axis_index("core"), lax.axis_index("y")
    x = lax.axis_index(("xh", "xl"))
    near, far = tiles(near_weight), tiles(far_weight[1::3])
    mine = jnp.where(
        core == 0, jnp.concatenate([near[:14], far[:4]], 0), jnp.concatenate([near[14:], far[4:]], 0)
    )
    plane = along_z(mine)
    spot = jnp.stack([core, x, y]).astype(jnp.int32)
    plane, spot, _ = lax.optimization_barrier((plane, spot, payload))
    parts = [plane] + [shift(plane, "y", d) for d in (1, 2, 3)]
    me = jnp.where(core == 0, y, x)
    which = [(me - j) % 4 for j in range(4)]
    whole = in_order([part[:, :EARLY] for part in parts], which)
    late = [in_order([part[:, EARLY:] for part in parts], which)]
    low, high, late[0] = lax.optimization_barrier((whole[:2], whole[2:], late[0]))
    behind, ahead = [shift(low, "x", 1)], [shift(high, "x", 3)]
    behind.append(shift(high, "x", 1))
    ahead.insert(0, shift(low, "x", 3))
    late += [shift(late[0], "x", d) for d in (1, 3, 2)]
    early = [low, high] + behind + ahead + [shift(behind[0], "x", 1), shift(ahead[1], "x", 3)]
    pieces = [early, late]
    for piece in pieces:
        count = len(piece)
        for i in range(count):
            piece.append(send(piece[i], "core", [(0, 1), (1, 0)]))
    return pieces, spot


def section(features, block_mask, near_weight, far_weight):
    active = jnp.repeat(jnp.repeat(jnp.repeat(block_mask, B, 0), B, 1), B, 2).astype(F32)
    masked = active[..., None] * features
    flags = jnp.pad(active.reshape(32, 1, 28), ((0, 0), (0, 3), (0, 228)))
    payload = jnp.concatenate([masked.reshape(32, 28, 256), flags], 1)
    (early, late), spot = gather(near_weight, far_weight, payload)
    received = lax.all_to_all(payload, GROUP, 0, 0, tiled=True)
    rows = ((3, 4 * PLANE, 768), BF16)
    acc = ((2, 4 * PLANE, 128), F32)
    hidden, middle = call(
        near_body,
        (spot, received),
        early,
        [acc, ((256, 768), BF16)],
        [rows, acc, ((4 * PLANE, 128), F32)],
        5_000_000_000,
    )
    (result,) = call(far_body, (spot, hidden, middle), late, [((32, 32, 256), F32)], [rows, acc], 2_000_000_000)
    back = lax.all_to_all(result, GROUP, 0, 0, tiled=True)
    back = back[:, :28].reshape(16, 2, 28, 256)
    return active[..., None] * (active[..., None] * features + back)


def solution(mesh):
    fine = Mesh(mesh.devices.reshape(2, 2, 4, 2, 2, 4), AXES)
    z, xy = ("zl", "core"), ("y", "xh", "xl", "zh")
    in_specs = (P(z, xy, None, None), P(z, xy, None), P(None, None, xy), P(None, None, xy))
    return jax.shard_map(section, mesh=fine, in_specs=in_specs, out_specs=P(z, xy, None, None), check_vma=False)
```

profile of v0, /device:TPU:3, one launch (start us, length us, event | category | flops | bytes accessed | tf_op | source)
XLA Modules:
  0.0 121.6 jit_solution(15307635247553407790)
XLA Ops:
  0.0 0.9 slice_bitcast_fusion
  2.5 5.7 %collective-permute-start = (f32[18,8,128]{2,1,0:T(8,128)S(1)}, f32[18,8,128]{2,1,0:T(8,128)S(1)}, u32[]{:S(2)}, u32[]{:S(2)}) collective-permute-start(f32[18,8,128]{2,1,0:T(8,128)S(1)} %maximum_select_fusion), channel_id=1, source_target_pairs={{0,131},{128,1},{1,128},{129,2},{2,129},{130,3},{3,130},{131,0},{4... | collective-permute-start | bytes 221192 | tf_op jit(solution)/shard_map/ppermute | solution.py:172
  8.2 1.2 collective-permute-start.1
  9.4 1.0 collective-permute-start.2
  12.2 1.1 select_maximum_fusion
  14.0 1.6 %collective-permute-done.2 = f32[18,8,128]{2,1,0:T(8,128)S(1)} collective-permute-done((f32[18,8,128]{2,1,0:T(8,128)S(1)}, f32[18,8,128]{2,1,0:T(8,128)S(1)}, u32[]{:S(2)}, u32[]{:S(2)}) %collective-permute-start.2) | collective-permute-done | bytes 73760 | tf_op jit(solution)/shard_map/ppermute | solution.py:172
  15.6 1.3 %collective-permute-start.3 = (f32[4,18,8,128]{3,2,1,0:T(8,128)S(1)}, f32[4,18,8,128]{3,2,1,0:T(8,128)S(1)}, u32[]{:S(2)}, u32[]{:S(2)}) collective-permute-start(f32[4,18,8,128]{3,2,1,0:T(8,128)S(1)} %pad_maximum_fusion.2), channel_id=1, source_target_pairs={{0,16},{4,20},{8,24},{12,28},{16,32},{20,36},{24,40},{28,44},{32,4... | collective-permute-start | bytes 884744 | tf_op jit(solution)/shard_map/ppermute | solution.py:172
  16.9 0.8 collective-permute-start.4
  17.8 1.9 %collective-permute-start.5 = (f32[4,18,8,128]{3,2,1,0:T(8,128)S(1)}, f32[4,18,8,128]{3,2,1,0:T(8,128)S(1)}, u32[]{:S(2)}, u32[]{:S(2)}) collective-permute-start(f32[4,18,8,128]{3,2,1,0:T(8,128)S(1)} %pad_maximum_fusion.2), channel_id=1, source_target_pairs={{0,48},{4,52},{8,56},{12,60},{16,0},{20,4},{24,8},{28,12},{32,16},... | collective-permute-start | bytes 884744 | tf_op jit(solution)/shard_map/ppermute | solution.py:172
  19.6 8.4 %all-to-all-start = ((f32[32,32,256]{2,1,0:T(8,128)}), f32[32,32,256]{2,1,0:T(8,128)S(1)}, u32[]{:S(2)}, u32[]{:S(2)}) async-start(f32[32,32,256]{2,1,0:T(8,128)} %select_maximum_fusion), calls=%async_computation | async-start | bytes 2097152 | tf_op jit(solution)/shard_map/all_to_all | solution.py:246
  28.5 1.4 %collective-permute-start.20 = (f32[4,4,4,8,128]{4,3,2,1,0:T(8,128)S(1)}, f32[4,4,4,8,128]{4,3,2,1,0:T(8,128)S(1)}, u32[]{:S(2)}, u32[]{:S(2)}) collective-permute-start(f32[4,4,4,8,128]{4,3,2,1,0:T(8,128)S(1)} %pad_maximum_fusion.3.refs_0_), channel_id=1, source_target_pairs={{0,4},{4,8},{8,12},{12,0},{16,20},{20,24},{24,28},{28,16},{32,36},... | collective-permute-start | bytes 786440 | tf_op jit(solution)/shard_map/ppermute | solution.py:172
  29.9 1.3 %collective-permute-start.21 = (f32[4,4,4,8,128]{4,3,2,1,0:T(8,128)S(1)}, f32[4,4,4,8,128]{4,3,2,1,0:T(8,128)}, u32[]{:S(2)}, u32[]{:S(2)}) collective-permute-start(f32[4,4,4,8,128]{4,3,2,1,0:T(8,128)S(1)} %pad_maximum_fusion.3.refs_0_), channel_id=1, source_target_pairs={{0,12},{4,0},{8,4},{12,8},{16,28},{20,16},{24,20},{28,24},{32,44},... | collective-permute-start | bytes 786440 | tf_op jit(solution)/shard_map/ppermute | solution.py:172
  31.4 2.5 %collective-permute-start.9 = (f32[2,4,14,8,128]{4,3,2,1,0:T(8,128)S(1)}, f32[2,4,14,8,128]{4,3,2,1,0:T(8,128)S(1)}, u32[]{:S(2)}, u32[]{:S(2)}) collective-permute-start(f32[2,4,14,8,128]{4,3,2,1,0:T(8,128)S(1)} %get-tuple-element.15.refs_1_), channel_id=1, source_target_pairs={{0,12},{4,0},{8,4},{12,8},{16,28},{20,16},{24,20},{28,24},{32,44},... | collective-permute-start | bytes 1376264 | tf_op jit(solution)/shard_map/ppermute | solution.py:172
  33.9 11.7 %collective-permute-done.20.refs_1_ = f32[4,4,4,8,128]{4,3,2,1,0:T(8,128)S(1)} collective-permute-done((f32[4,4,4,8,128]{4,3,2,1,0:T(8,128)S(1)}, f32[4,4,4,8,128]{4,3,2,1,0:T(8,128)S(1)}, u32[]{:S(2)}, u32[]{:S(2)}) %collective-permute-start.20) | collective-permute-done | bytes 262176 | tf_op jit(solution)/shard_map/ppermute | solution.py:172
  46.5 12.3 %collective-permute-done.22.refs_3_ = f32[4,4,4,8,128]{4,3,2,1,0:T(8,128)} collective-permute-done((f32[4,4,4,8,128]{4,3,2,1,0:T(8,128)S(1)}, f32[4,4,4,8,128]{4,3,2,1,0:T(8,128)}, u32[]{:S(2)}, u32[]{:S(2)}) %collective-permute-start.22) | collective-permute-done | bytes 262176 | tf_op jit(solution)/shard_map/ppermute | solution.py:172
  58.8 1.3 %collective-permute-start.12 = (f32[2,4,14,8,128]{4,3,2,1,0:T(8,128)S(1)}, f32[2,4,14,8,128]{4,3,2,1,0:T(8,128)S(1)}, u32[]{:S(2)}, u32[]{:S(2)}) collective-permute-start(f32[2,4,14,8,128]{4,3,2,1,0:T(8,128)S(1)} %get-tuple-element.14.refs_0_), channel_id=1, source_target_pairs={{0,64},{64,0},{1,65},{65,1},{2,66},{66,2},{3,67},{67,3},{4,68},{68... | collective-permute-start | bytes 1376264 | tf_op jit(solution)/shard_map/ppermute | solution.py:172
  61.2 2.0 %collective-permute-start.11 = (f32[2,4,14,8,128]{4,3,2,1,0:T(8,128)S(1)}, f32[2,4,14,8,128]{4,3,2,1,0:T(8,128)S(1)}, u32[]{:S(2)}, u32[]{:S(2)}) collective-permute-start(f32[2,4,14,8,128]{4,3,2,1,0:T(8,128)S(1)} %collective-permute-done.9.refs_5_), channel_id=1, source_target_pairs={{0,12},{4,0},{8,4},{12,8},{16,28},{20,16},{24,20},{28,24},{32,44},... | collective-permute-start | bytes 1376264 | tf_op jit(solution)/shard_map/ppermute | solution.py:172
  63.8 5.1 %collective-permute-done.10.refs_6_ = f32[2,4,14,8,128]{4,3,2,1,0:T(8,128)S(1)} collective-permute-done((f32[2,4,14,8,128]{4,3,2,1,0:T(8,128)S(1)}, f32[2,4,14,8,128]{4,3,2,1,0:T(8,128)S(1)}, u32[]{:S(2)}, u32[]{:S(2)}) %collective-permute-start.10) | collective-permute-done | bytes 458784 | tf_op jit(solution)/shard_map/ppermute | solution.py:172
  69.4 1.0 collective-permute-start.18
  72.7 1.0 copy-done.1
  73.7 12.7 %shard_map.46 = (f32[2,896,128]{2,1,0:T(8,128)}, bf16[256,768]{1,0:T(8,128)(2,1)}) custom-call(s32[3]{0:T(128)} %pad_add_fusion.spot, f32[32,32,256]{2,1,0:T(8,128)} %copy-done.1, f32[2,4,14,8,128]{4,3,2,1,0:T(8,128)} %copy-done.2, f32[2,4,14,8,128]{4,3,2,1,0:T(8,128)} %copy-done.3, f32[2,4,14,8,128]{4,3,2,1,0:T(8,128)} %copy-done.5, ...), custom_call_target="tpu_custom_call" | custom-call | flops 5000000000 | bytes 8000000 | tf_op jit(solution)/shard_map/pallas_call | solution.py:156
  86.4 6.9 %shard_map.47 = f32[32,32,256]{2,1,0:T(8,128)} custom-call(s32[3]{0:T(128)} %pad_add_fusion.spot, f32[2,896,128]{2,1,0:T(8,128)} %get-tuple-element.16.hidden, bf16[256,768]{1,0:T(8,128)(2,1)} %get-tuple-element.17.middle, f32[4,4,4,8,128]{4,3,2,1,0:T(8,128)} %copy-done.4, f32[4,4,4,8,128]{4,3,2,1,0:T(8,128)} %copy-done.18, ...), custom_call_target="tpu_custom_call" | custom-call | flops 2000000000 | bytes 8000000 | tf_op jit(solution)/shard_map/pallas_call | solution.py:156
  93.3 26.7 %all_to_all.10 = f32[32,32,256]{2,1,0:T(8,128)S(1)} all-to-all(f32[32,32,256]{2,1,0:T(8,128)} %shard_map.47), channel_id=1, replica_groups=mesh['zl'=2,'core'=2,'y'=4,'xh'=2,'xl'=2,'zh'=4] {'zl','core','y','xh'}, dimensions={0} | all-to-all | bytes 2097152 | tf_op jit(solution)/shard_map/all_to_all | solution.py:258
  120.0 1.6 %fusion = f32[16,2,28,256]{3,1,2,0:T(2,128)} fusion(f32[16,2,28,256]{3,2,1,0:T(8,128)S(1)} %bitcast.56, f32[16,28]{1,0:T(8,128)S(1)} %copy.20, f32[16,2,28,256]{3,1,2,0:T(2,128)S(1)} %copy-done), kind=kLoop, calls=%fused_computation.3 | loop fusion | flops 688128 | bytes 2754304 | tf_op jit(solution)/shard_map/mul | solution.py:260
  (101 shorter events, 9.8 us)
Async XLA Ops:
  2.5 11.5 %collective-permute-start = (f32[18,8,128]{2,1,0:T(8,128)S(1)}, f32[18,8,128]{2,1,0:T(8,128)S(1)}, u32[]{:S(2)}, u32[]{:S(2)}) collective-permute-start(f32[18,8,128]{2,1,0:T(8,128)S(1)} %maximum_select_fusion), channel_id=1, source_target_pairs={{0,131},{128,1},{1,128},{129,2},{2,129},{130,3},{3,130},{131,0},{4... | collective-permute-start | bytes 221192 | tf_op jit(solution)/shard_map/ppermute | solution.py:172
  8.2 5.8 %collective-permute-start.1 = (f32[18,8,128]{2,1,0:T(8,128)S(1)}, f32[18,8,128]{2,1,0:T(8,128)S(1)}, u32[]{:S(2)}, u32[]{:S(2)}) collective-permute-start(f32[18,8,128]{2,1,0:T(8,128)S(1)} %maximum_select_fusion), channel_id=1, source_target_pairs={{0,3},{128,129},{1,0},{129,130},{2,1},{130,131},{3,2},{131,128},{4... | collective-permute-start | bytes 221192 | tf_op jit(solution)/shard_map/ppermute | solution.py:172
  9.4 6.2 %collective-permute-start.2 = (f32[18,8,128]{2,1,0:T(8,128)S(1)}, f32[18,8,128]{2,1,0:T(8,128)S(1)}, u32[]{:S(2)}, u32[]{:S(2)}) collective-permute-start(f32[18,8,128]{2,1,0:T(8,128)S(1)} %maximum_select_fusion), channel_id=1, source_target_pairs={{0,130},{128,2},{1,131},{129,3},{2,128},{130,0},{3,129},{131,1},{4... | collective-permute-start | bytes 221192 | tf_op jit(solution)/shard_map/ppermute | solution.py:172
  15.6 12.5 %collective-permute-start.3 = (f32[4,18,8,128]{3,2,1,0:T(8,128)S(1)}, f32[4,18,8,128]{3,2,1,0:T(8,128)S(1)}, u32[]{:S(2)}, u32[]{:S(2)}) collective-permute-start(f32[4,18,8,128]{3,2,1,0:T(8,128)S(1)} %pad_maximum_fusion.2), channel_id=1, source_target_pairs={{0,16},{4,20},{8,24},{12,28},{16,32},{20,36},{24,40},{28,44},{32,4... | collective-permute-start | bytes 884744 | tf_op jit(solution)/shard_map/ppermute | solution.py:172
  16.9 11.2 %collective-permute-start.4 = (f32[4,18,8,128]{3,2,1,0:T(8,128)S(1)}, f32[4,18,8,128]{3,2,1,0:T(8,128)S(1)}, u32[]{:S(2)}, u32[]{:S(2)}) collective-permute-start(f32[4,18,8,128]{3,2,1,0:T(8,128)S(1)} %pad_maximum_fusion.2), channel_id=1, source_target_pairs={{0,32},{4,36},{8,40},{12,44},{16,48},{20,52},{24,56},{28,60},{32,0... | collective-permute-start | bytes 884744 | tf_op jit(solution)/shard_map/ppermute | solution.py:172
  17.8 10.4 %collective-permute-start.5 = (f32[4,18,8,128]{3,2,1,0:T(8,128)S(1)}, f32[4,18,8,128]{3,2,1,0:T(8,128)S(1)}, u32[]{:S(2)}, u32[]{:S(2)}) collective-permute-start(f32[4,18,8,128]{3,2,1,0:T(8,128)S(1)} %pad_maximum_fusion.2), channel_id=1, source_target_pairs={{0,48},{4,52},{8,56},{12,60},{16,0},{20,4},{24,8},{28,12},{32,16},... | collective-permute-start | bytes 884744 | tf_op jit(solution)/shard_map/ppermute | solution.py:172
  19.6 53.0 %all-to-all-start = ((f32[32,32,256]{2,1,0:T(8,128)}), f32[32,32,256]{2,1,0:T(8,128)S(1)}, u32[]{:S(2)}, u32[]{:S(2)}) async-start(f32[32,32,256]{2,1,0:T(8,128)} %select_maximum_fusion), calls=%async_computation | async-start | bytes 2097152 | tf_op jit(solution)/shard_map/all_to_all | solution.py:246
  28.5 17.2 %collective-permute-start.20 = (f32[4,4,4,8,128]{4,3,2,1,0:T(8,128)S(1)}, f32[4,4,4,8,128]{4,3,2,1,0:T(8,128)S(1)}, u32[]{:S(2)}, u32[]{:S(2)}) collective-permute-start(f32[4,4,4,8,128]{4,3,2,1,0:T(8,128)S(1)} %pad_maximum_fusion.3.refs_0_), channel_id=1, source_target_pairs={{0,4},{4,8},{8,12},{12,0},{16,20},{20,24},{24,28},{28,16},{32,36},... | collective-permute-start | bytes 786440 | tf_op jit(solution)/shard_map/ppermute | solution.py:172
  29.9 16.4 %collective-permute-start.21 = (f32[4,4,4,8,128]{4,3,2,1,0:T(8,128)S(1)}, f32[4,4,4,8,128]{4,3,2,1,0:T(8,128)}, u32[]{:S(2)}, u32[]{:S(2)}) collective-permute-start(f32[4,4,4,8,128]{4,3,2,1,0:T(8,128)S(1)} %pad_maximum_fusion.3.refs_0_), channel_id=1, source_target_pairs={{0,12},{4,0},{8,4},{12,8},{16,28},{20,16},{24,20},{28,24},{32,44},... | collective-permute-start | bytes 786440 | tf_op jit(solution)/shard_map/ppermute | solution.py:172
  31.2 28.8 %collective-permute-start.6 = (f32[2,4,14,8,128]{4,3,2,1,0:T(8,128)S(1)}, f32[2,4,14,8,128]{4,3,2,1,0:T(8,128)S(1)}, u32[]{:S(2)}, u32[]{:S(2)}) collective-permute-start(f32[2,4,14,8,128]{4,3,2,1,0:T(8,128)S(1)} %get-tuple-element.14.refs_0_), channel_id=1, source_target_pairs={{0,4},{4,8},{8,12},{12,0},{16,20},{20,24},{24,28},{28,16},{32,36},... | collective-permute-start | bytes 1376264 | tf_op jit(solution)/shard_map/ppermute | solution.py:172
  31.4 29.0 %collective-permute-start.9 = (f32[2,4,14,8,128]{4,3,2,1,0:T(8,128)S(1)}, f32[2,4,14,8,128]{4,3,2,1,0:T(8,128)S(1)}, u32[]{:S(2)}, u32[]{:S(2)}) collective-permute-start(f32[2,4,14,8,128]{4,3,2,1,0:T(8,128)S(1)} %get-tuple-element.15.refs_1_), channel_id=1, source_target_pairs={{0,12},{4,0},{8,4},{12,8},{16,28},{20,16},{24,20},{28,24},{32,44},... | collective-permute-start | bytes 1376264 | tf_op jit(solution)/shard_map/ppermute | solution.py:172
  33.9 27.2 %collective-permute-start.7 = (f32[2,4,14,8,128]{4,3,2,1,0:T(8,128)S(1)}, f32[2,4,14,8,128]{4,3,2,1,0:T(8,128)S(1)}, u32[]{:S(2)}, u32[]{:S(2)}) collective-permute-start(f32[2,4,14,8,128]{4,3,2,1,0:T(8,128)S(1)} %get-tuple-element.15.refs_1_), channel_id=1, source_target_pairs={{0,4},{4,8},{8,12},{12,0},{16,20},{20,24},{24,28},{28,16},{32,36},... | collective-permute-start | bytes 1376264 | tf_op jit(solution)/shard_map/ppermute | solution.py:172
  45.6 17.5 %collective-permute-start.8 = (f32[2,4,14,8,128]{4,3,2,1,0:T(8,128)S(1)}, f32[2,4,14,8,128]{4,3,2,1,0:T(8,128)S(1)}, u32[]{:S(2)}, u32[]{:S(2)}) collective-permute-start(f32[2,4,14,8,128]{4,3,2,1,0:T(8,128)S(1)} %get-tuple-element.14.refs_0_), channel_id=1, source_target_pairs={{0,12},{4,0},{8,4},{12,8},{16,28},{20,16},{24,20},{28,24},{32,44},... | collective-permute-start | bytes 1376264 | tf_op jit(solution)/shard_map/ppermute | solution.py:172
  46.3 12.4 %collective-permute-start.22 = (f32[4,4,4,8,128]{4,3,2,1,0:T(8,128)S(1)}, f32[4,4,4,8,128]{4,3,2,1,0:T(8,128)}, u32[]{:S(2)}, u32[]{:S(2)}) collective-permute-start(f32[4,4,4,8,128]{4,3,2,1,0:T(8,128)S(1)} %pad_maximum_fusion.3.refs_0_), channel_id=1, source_target_pairs={{0,8},{4,12},{8,0},{12,4},{16,24},{20,28},{24,16},{28,20},{32,40},... | collective-permute-start | bytes 786440 | tf_op jit(solution)/shard_map/ppermute | solution.py:172
  58.8 4.4 %collective-permute-start.12 = (f32[2,4,14,8,128]{4,3,2,1,0:T(8,128)S(1)}, f32[2,4,14,8,128]{4,3,2,1,0:T(8,128)S(1)}, u32[]{:S(2)}, u32[]{:S(2)}) collective-permute-start(f32[2,4,14,8,128]{4,3,2,1,0:T(8,128)S(1)} %get-tuple-element.14.refs_0_), channel_id=1, source_target_pairs={{0,64},{64,0},{1,65},{65,1},{2,66},{66,2},{3,67},{67,3},{4,68},{68... | collective-permute-start | bytes 1376264 | tf_op jit(solution)/shard_map/ppermute | solution.py:172
  60.4 8.6 %collective-permute-start.10 = (f32[2,4,14,8,128]{4,3,2,1,0:T(8,128)S(1)}, f32[2,4,14,8,128]{4,3,2,1,0:T(8,128)S(1)}, u32[]{:S(2)}, u32[]{:S(2)}) collective-permute-start(f32[2,4,14,8,128]{4,3,2,1,0:T(8,128)S(1)} %collective-permute-done.6.refs_2_), channel_id=1, source_target_pairs={{0,4},{4,8},{8,12},{12,0},{16,20},{20,24},{24,28},{28,16},{32,36},... | collective-permute-start | bytes 1376264 | tf_op jit(solution)/shard_map/ppermute | solution.py:172
  61.2 8.2 %collective-permute-start.11 = (f32[2,4,14,8,128]{4,3,2,1,0:T(8,128)S(1)}, f32[2,4,14,8,128]{4,3,2,1,0:T(8,128)S(1)}, u32[]{:S(2)}, u32[]{:S(2)}) collective-permute-start(f32[2,4,14,8,128]{4,3,2,1,0:T(8,128)S(1)} %collective-permute-done.9.refs_5_), channel_id=1, source_target_pairs={{0,12},{4,0},{8,4},{12,8},{16,28},{20,16},{24,20},{28,24},{32,44},... | collective-permute-start | bytes 1376264 | tf_op jit(solution)/shard_map/ppermute | solution.py:172
  63.2 7.2 %collective-permute-start.14 = (f32[2,4,14,8,128]{4,3,2,1,0:T(8,128)S(1)}, f32[2,4,14,8,128]{4,3,2,1,0:T(8,128)S(1)}, u32[]{:S(2)}, u32[]{:S(2)}) collective-permute-start(f32[2,4,14,8,128]{4,3,2,1,0:T(8,128)S(1)} %collective-permute-done.6.refs_2_), channel_id=1, source_target_pairs={{0,64},{64,0},{1,65},{65,1},{2,66},{66,2},{3,67},{67,3},{4,68},{68... | collective-permute-start | bytes 1376264 | tf_op jit(solution)/shard_map/ppermute | solution.py:172
  63.2 7.3 %collective-permute-start.15 = (f32[2,4,14,8,128]{4,3,2,1,0:T(8,128)S(1)}, f32[2,4,14,8,128]{4,3,2,1,0:T(8,128)S(1)}, u32[]{:S(2)}, u32[]{:S(2)}) collective-permute-start(f32[2,4,14,8,128]{4,3,2,1,0:T(8,128)S(1)} %collective-permute-done.7.refs_3_), channel_id=1, source_target_pairs={{0,64},{64,0},{1,65},{65,1},{2,66},{66,2},{3,67},{67,3},{4,68},{68... | collective-permute-start | bytes 1376264 | tf_op jit(solution)/shard_map/ppermute | solution.py:172
  63.7 7.3 %collective-permute-start.16 = (f32[2,4,14,8,128]{4,3,2,1,0:T(8,128)S(1)}, f32[2,4,14,8,128]{4,3,2,1,0:T(8,128)S(1)}, u32[]{:S(2)}, u32[]{:S(2)}) collective-permute-start(f32[2,4,14,8,128]{4,3,2,1,0:T(8,128)S(1)} %collective-permute-done.8.refs_4_), channel_id=1, source_target_pairs={{0,64},{64,0},{1,65},{65,1},{2,66},{66,2},{3,67},{67,3},{4,68},{68... | collective-permute-start | bytes 1376264 | tf_op jit(solution)/shard_map/ppermute | solution.py:172
  70.5 15.9 %collective-permute-start.23 = (f32[4,4,4,8,128]{4,3,2,1,0:T(8,128)S(1)}, f32[4,4,4,8,128]{4,3,2,1,0:T(8,128)}, u32[]{:S(2)}, u32[]{:S(2)}) collective-permute-start(f32[4,4,4,8,128]{4,3,2,1,0:T(8,128)S(1)} %pad_maximum_fusion.3.refs_0_), channel_id=1, source_target_pairs={{0,64},{64,0},{1,65},{65,1},{2,66},{66,2},{3,67},{67,3},{4,68},{68... | collective-permute-start | bytes 786440 | tf_op jit(solution)/shard_map/ppermute | solution.py:172
  71.0 15.4 %collective-permute-start.24 = (f32[4,4,4,8,128]{4,3,2,1,0:T(8,128)S(1)}, f32[4,4,4,8,128]{4,3,2,1,0:T(8,128)}, u32[]{:S(2)}, u32[]{:S(2)}) collective-permute-start(f32[4,4,4,8,128]{4,3,2,1,0:T(8,128)S(1)} %collective-permute-done.20.refs_1_), channel_id=1, source_target_pairs={{0,64},{64,0},{1,65},{65,1},{2,66},{66,2},{3,67},{67,3},{4,68},{68... | collective-permute-start | bytes 786440 | tf_op jit(solution)/shard_map/ppermute | solution.py:172
  71.1 15.3 %collective-permute-start.25 = (f32[4,4,4,8,128]{4,3,2,1,0:T(8,128)}, f32[4,4,4,8,128]{4,3,2,1,0:T(8,128)}, u32[]{:S(2)}, u32[]{:S(2)}) collective-permute-start(f32[4,4,4,8,128]{4,3,2,1,0:T(8,128)} %collective-permute-done.21.refs_2_), channel_id=1, source_target_pairs={{0,64},{64,0},{1,65},{65,1},{2,66},{66,2},{3,67},{67,3},{4,68},{68... | collective-permute-start | bytes 786440 | tf_op jit(solution)/shard_map/ppermute | solution.py:172
  71.8 14.6 %collective-permute-start.26 = (f32[4,4,4,8,128]{4,3,2,1,0:T(8,128)}, f32[4,4,4,8,128]{4,3,2,1,0:T(8,128)}, u32[]{:S(2)}, u32[]{:S(2)}) collective-permute-start(f32[4,4,4,8,128]{4,3,2,1,0:T(8,128)} %collective-permute-done.22.refs_3_), channel_id=1, source_target_pairs={{0,64},{64,0},{1,65},{65,1},{2,66},{66,2},{3,67},{67,3},{4,68},{68... | collective-permute-start | bytes 786440 | tf_op jit(solution)/shard_map/ppermute | solution.py:172
  (23 other events, 268.7 us)
where the time goes:
time: 122 us
  starting transfers between devices  34.1 us (28%)
  waiting for transfers between devices  31.4 us (26%)
  blocking collectives  26.7 us (22%)
  Pallas kernels  19.6 us (16%)
  other arithmetic  4.93 us (4%)
  local copies, waits for them, and re-layouts  4.54 us (4%)
    ppermute x27, waiting for transfers between devices, send(): return lax.ppermute(value, axis, pairs)  31.4 us
    all_to_all x1, blocking collectives, section(): back = lax.all_to_all(result, GROUP, 0, 0, tiled=True)  26.7 us
    ppermute x27, starting transfers between devices, send(): return lax.ppermute(value, axis, pairs)  25.7 us
    pallas_call x2, Pallas kernels, call(): pl.pallas_call(body, out_shape=[jax.ShapeDtypeStruct(shape, dtype) for sh...  19.6 us
    all_to_all x1, starting transfers between devices, section(): received = lax.all_to_all(payload, GROUP, 0, 0, tiled=True)  8.42 us
  transfers between devices with their start and end apart: 28, of which 6 were waited for; matrix products, arithmetic and copies ran while one was open for 3% of the time, Pallas kernels for 10%

commit v1 on v0

--- a/solution.py
+++ b/solution.py
@@ -227,14 +227,17 @@
     behind, ahead = [shift(low, "x", 1)], [shift(high, "x", 3)]
     behind.append(shift(high, "x", 1))
     ahead.insert(0, shift(low, "x", 3))
-    late += [shift(late[0], "x", d) for d in (1, 3, 2)]
+    late += [shift(late[0], "x", d) for d in (1, 3)]
+    late.append(shift(late[0], "x", 2))
     early = [low, high] + behind + ahead + [shift(behind[0], "x", 1), shift(ahead[1], "x", 3)]
+    received = lax.all_to_all(payload, GROUP, 0, 0, tiled=True)
+    received, early[0] = lax.optimization_barrier((received, early[0]))
     pieces = [early, late]
     for piece in pieces:
         count = len(piece)
         for i in range(count):
             piece.append(send(piece[i], "core", [(0, 1), (1, 0)]))
-    return pieces, spot
+    return pieces, spot, received
 
 
 def section(features, block_mask, near_weight, far_weight):
@@ -242,8 +245,7 @@
     masked = active[..., None] * features
     flags = jnp.pad(active.reshape(32, 1, 28), ((0, 0), (0, 3), (0, 228)))
     payload = jnp.concatenate([masked.reshape(32, 28, 256), flags], 1)
-    (early, late), spot = gather(near_weight, far_weight, payload)
-    received = lax.all_to_all(payload, GROUP, 0, 0, tiled=True)
+    (early, late), spot, received = gather(near_weight, far_weight, payload)
     rows = ((3, 4 * PLANE, 768), BF16)
     acc = ((2, 4 * PLANE, 128), F32)
     hidden, middle = call(

time: 122 us -> 122 us (level)
  transfers between devices with their start and end apart: 28 -> 28, of which waited for: 6 -> 8; matrix products, arithmetic and copies ran while one was open for 3% -> 3% of each run, Pallas kernels for 10% -> 11%
where the time goes in v1:
time: 122 us
  starting transfers between devices  34.1 us (28%)
  waiting for transfers between devices  31.9 us (26%)
  blocking collectives  26.7 us (22%)
  Pallas kernels  19.8 us (16%)
  other arithmetic  4.85 us (4%)
  local copies, waits for them, and re-layouts  3.92 us (3%)
    ppermute x27, waiting for transfers between devices, send(): return lax.ppermute(value, axis, pairs)  31.9 us
    all_to_all x1, blocking collectives, section(): back = lax.all_to_all(result, GROUP, 0, 0, tiled=True)  26.7 us
    ppermute x27, starting transfers between devices, send(): return lax.ppermute(value, axis, pairs)  25.7 us
    pallas_call x2, Pallas kernels, call(): pl.pallas_call(body, out_shape=[jax.ShapeDtypeStruct(shape, dtype) for sh...  19.8 us
    all_to_all x1, starting transfers between devices, gather(): received = lax.all_to_all(payload, GROUP, 0, 0, tiled=True)  8.42 us
  transfers between devices with their start and end apart: 28, of which 8 were waited for; matrix products, arithmetic and copies ran while one was open for 3% of the time, Pallas kernels for 11%

profile of v1, /device:TPU:3, one launch (start us, length us, event | category | flops | bytes accessed | tf_op | source)
XLA Modules:
  0.0 121.6 jit_solution(16194806785365525113)
XLA Ops:
  0.0 0.9 slice_bitcast_fusion
  0.9 0.8 slice.76
  2.5 5.7 %collective-permute-start = (f32[18,8,128]{2,1,0:T(8,128)S(1)}, f32[18,8,128]{2,1,0:T(8,128)S(1)}, u32[]{:S(2)}, u32[]{:S(2)}) collective-permute-start(f32[18,8,128]{2,1,0:T(8,128)S(1)} %maximum_select_fusion), channel_id=1, source_target_pairs={{0,131},{128,1},{1,128},{129,2},{2,129},{130,3},{3,130},{131,0},{4... | collective-permute-start | bytes 221192 | tf_op jit(solution)/shard_map/ppermute | solution.py:172
  8.2 1.2 collective-permute-start.1
  9.4 1.0 collective-permute-start.2
  12.2 1.1 select_maximum_fusion
  13.9 1.7 %collective-permute-done.2 = f32[18,8,128]{2,1,0:T(8,128)S(1)} collective-permute-done((f32[18,8,128]{2,1,0:T(8,128)S(1)}, f32[18,8,128]{2,1,0:T(8,128)S(1)}, u32[]{:S(2)}, u32[]{:S(2)}) %collective-permute-start.2) | collective-permute-done | bytes 73760 | tf_op jit(solution)/shard_map/ppermute | solution.py:172
  15.6 1.3 %collective-permute-start.3 = (f32[4,18,8,128]{3,2,1,0:T(8,128)S(1)}, f32[4,18,8,128]{3,2,1,0:T(8,128)S(1)}, u32[]{:S(2)}, u32[]{:S(2)}) collective-permute-start(f32[4,18,8,128]{3,2,1,0:T(8,128)S(1)} %pad_maximum_fusion.2), channel_id=1, source_target_pairs={{0,16},{4,20},{8,24},{12,28},{16,32},{20,36},{24,40},{28,44},{32,4... | collective-permute-start | bytes 884744 | tf_op jit(solution)/shard_map/ppermute | solution.py:172
  16.9 0.8 collective-permute-start.4
  17.8 1.9 %collective-permute-start.5 = (f32[4,18,8,128]{3,2,1,0:T(8,128)S(1)}, f32[4,18,8,128]{3,2,1,0:T(8,128)S(1)}, u32[]{:S(2)}, u32[]{:S(2)}) collective-permute-start(f32[4,18,8,128]{3,2,1,0:T(8,128)S(1)} %pad_maximum_fusion.2), channel_id=1, source_target_pairs={{0,48},{4,52},{8,56},{12,60},{16,0},{20,4},{24,8},{28,12},{32,16},... | collective-permute-start | bytes 884744 | tf_op jit(solution)/shard_map/ppermute | solution.py:172
  19.6 8.4 %all-to-all-start = ((f32[32,32,256]{2,1,0:T(8,128)}), f32[32,32,256]{2,1,0:T(8,128)S(1)}, u32[]{:S(2)}, u32[]{:S(2)}) async-start(f32[32,32,256]{2,1,0:T(8,128)} %select_maximum_fusion), calls=%async_computation | async-start | bytes 2097152 | tf_op jit(solution)/shard_map/all_to_all | solution.py:233
  28.5 1.4 %collective-permute-start.20 = (f32[4,4,4,8,128]{4,3,2,1,0:T(8,128)S(1)}, f32[4,4,4,8,128]{4,3,2,1,0:T(8,128)S(1)}, u32[]{:S(2)}, u32[]{:S(2)}) collective-permute-start(f32[4,4,4,8,128]{4,3,2,1,0:T(8,128)S(1)} %pad_maximum_fusion.3.refs_0_), channel_id=1, source_target_pairs={{0,4},{4,8},{8,12},{12,0},{16,20},{20,24},{24,28},{28,16},{32,36},... | collective-permute-start | bytes 786440 | tf_op jit(solution)/shard_map/ppermute | solution.py:172
  29.9 1.3 %collective-permute-start.21 = (f32[4,4,4,8,128]{4,3,2,1,0:T(8,128)S(1)}, f32[4,4,4,8,128]{4,3,2,1,0:T(8,128)S(1)}, u32[]{:S(2)}, u32[]{:S(2)}) collective-permute-start(f32[4,4,4,8,128]{4,3,2,1,0:T(8,128)S(1)} %pad_maximum_fusion.3.refs_0_), channel_id=1, source_target_pairs={{0,12},{4,0},{8,4},{12,8},{16,28},{20,16},{24,20},{28,24},{32,44},... | collective-permute-start | bytes 786440 | tf_op jit(solution)/shard_map/ppermute | solution.py:172
  31.4 2.5 %collective-permute-start.9 = (f32[2,4,14,8,128]{4,3,2,1,0:T(8,128)S(1)}, f32[2,4,14,8,128]{4,3,2,1,0:T(8,128)}, u32[]{:S(2)}, u32[]{:S(2)}) collective-permute-start(f32[2,4,14,8,128]{4,3,2,1,0:T(8,128)S(1)} %get-tuple-element.19.refs_1_), channel_id=1, source_target_pairs={{0,12},{4,0},{8,4},{12,8},{16,28},{20,16},{24,20},{28,24},{32,44},... | collective-permute-start | bytes 1376264 | tf_op jit(solution)/shard_map/ppermute | solution.py:172
  33.9 11.7 %collective-permute-done.20.refs_1_ = f32[4,4,4,8,128]{4,3,2,1,0:T(8,128)S(1)} collective-permute-done((f32[4,4,4,8,128]{4,3,2,1,0:T(8,128)S(1)}, f32[4,4,4,8,128]{4,3,2,1,0:T(8,128)S(1)}, u32[]{:S(2)}, u32[]{:S(2)}) %collective-permute-start.20) | collective-permute-done | bytes 262176 | tf_op jit(solution)/shard_map/ppermute | solution.py:172
  46.4 12.3 %collective-permute-done.22.refs_3_ = f32[4,4,4,8,128]{4,3,2,1,0:T(8,128)S(1)} collective-permute-done((f32[4,4,4,8,128]{4,3,2,1,0:T(8,128)S(1)}, f32[4,4,4,8,128]{4,3,2,1,0:T(8,128)S(1)}, u32[]{:S(2)}, u32[]{:S(2)}) %collective-permute-start.22) | collective-permute-done | bytes 262176 | tf_op jit(solution)/shard_map/ppermute | solution.py:172
  58.6 1.3 %collective-permute-start.13 = (f32[2,4,14,8,128]{4,3,2,1,0:T(8,128)S(1)}, f32[2,4,14,8,128]{4,3,2,1,0:T(8,128)}, u32[]{:S(2)}, u32[]{:S(2)}) collective-permute-start(f32[2,4,14,8,128]{4,3,2,1,0:T(8,128)S(1)} %get-tuple-element.19.refs_1_), channel_id=1, source_target_pairs={{0,64},{64,0},{1,65},{65,1},{2,66},{66,2},{3,67},{67,3},{4,68},{68... | collective-permute-start | bytes 1376264 | tf_op jit(solution)/shard_map/ppermute | solution.py:172
  60.8 2.0 %collective-permute-start.11 = (f32[2,4,14,8,128]{4,3,2,1,0:T(8,128)}, f32[2,4,14,8,128]{4,3,2,1,0:T(8,128)}, u32[]{:S(2)}, u32[]{:S(2)}) collective-permute-start(f32[2,4,14,8,128]{4,3,2,1,0:T(8,128)} %collective-permute-done.9.refs_5_), channel_id=1, source_target_pairs={{0,12},{4,0},{8,4},{12,8},{16,28},{20,16},{24,20},{28,24},{32,44},... | collective-permute-start | bytes 1376264 | tf_op jit(solution)/shard_map/ppermute | solution.py:172
  64.2 4.7 %collective-permute-done.10.refs_6_ = f32[2,4,14,8,128]{4,3,2,1,0:T(8,128)} collective-permute-done((f32[2,4,14,8,128]{4,3,2,1,0:T(8,128)}, f32[2,4,14,8,128]{4,3,2,1,0:T(8,128)}, u32[]{:S(2)}, u32[]{:S(2)}) %collective-permute-start.10) | collective-permute-done | bytes 458784 | tf_op jit(solution)/shard_map/ppermute | solution.py:172
  69.3 1.0 collective-permute-start.18
  73.4 12.9 %shard_map.46 = (f32[2,896,128]{2,1,0:T(8,128)}, bf16[256,768]{1,0:T(8,128)(2,1)}) custom-call(s32[3]{0:T(128)} %pad_add_fusion.spot, f32[32,32,256]{2,1,0:T(8,128)} %copy-done.1, f32[2,4,14,8,128]{4,3,2,1,0:T(8,128)} %copy-done.2, f32[2,4,14,8,128]{4,3,2,1,0:T(8,128)} %copy-done.3, f32[2,4,14,8,128]{4,3,2,1,0:T(8,128)} %collective-permute-done.6.refs_2_, ...), custom_call_target="tpu_custom_call" | custom-call | flops 5000000000 | bytes 8000000 | tf_op jit(solution)/shard_map/pallas_call | solution.py:156
  86.4 6.9 %shard_map.47 = f32[32,32,256]{2,1,0:T(8,128)} custom-call(s32[3]{0:T(128)} %pad_add_fusion.spot, f32[2,896,128]{2,1,0:T(8,128)} %get-tuple-element.20.hidden, bf16[256,768]{1,0:T(8,128)(2,1)} %get-tuple-element.21.middle, f32[4,4,4,8,128]{4,3,2,1,0:T(8,128)} %copy-done.4, f32[4,4,4,8,128]{4,3,2,1,0:T(8,128)} %copy-done.7, f32[4,4,4,8,128]{4,3,2,1,0:T(8,128)} %copy-done.8, ...), custom_call_target="tpu_custom_call" | custom-call | flops 2000000000 | bytes 8000000 | tf_op jit(solution)/shard_map/pallas_call | solution.py:156
  93.2 26.7 %all_to_all.10 = f32[32,32,256]{2,1,0:T(8,128)S(1)} all-to-all(f32[32,32,256]{2,1,0:T(8,128)} %shard_map.47), channel_id=1, replica_groups=mesh['zl'=2,'core'=2,'y'=4,'xh'=2,'xl'=2,'zh'=4] {'zl','core','y','xh'}, dimensions={0} | all-to-all | bytes 2097152 | tf_op jit(solution)/shard_map/all_to_all | solution.py:260
  120.0 1.7 %fusion = f32[16,2,28,256]{3,1,2,0:T(2,128)} fusion(f32[16,2,28,256]{3,2,1,0:T(8,128)S(1)} %bitcast.56, f32[16,28]{1,0:T(8,128)S(1)} %copy.20, f32[16,2,28,256]{3,1,2,0:T(2,128)S(1)} %copy-done), kind=kLoop, calls=%fused_computation.3 | loop fusion | flops 688128 | bytes 2754304 | tf_op jit(solution)/shard_map/mul | solution.py:262
  (83 shorter events, 10.1 us)
Async XLA Ops:
  2.5 11.4 %collective-permute-start = (f32[18,8,128]{2,1,0:T(8,128)S(1)}, f32[18,8,128]{2,1,0:T(8,128)S(1)}, u32[]{:S(2)}, u32[]{:S(2)}) collective-permute-start(f32[18,8,128]{2,1,0:T(8,128)S(1)} %maximum_select_fusion), channel_id=1, source_target_pairs={{0,131},{128,1},{1,128},{129,2},{2,129},{130,3},{3,130},{131,0},{4... | collective-permute-start | bytes 221192 | tf_op jit(solution)/shard_map/ppermute | solution.py:172
  8.2 5.7 %collective-permute-start.1 = (f32[18,8,128]{2,1,0:T(8,128)S(1)}, f32[18,8,128]{2,1,0:T(8,128)S(1)}, u32[]{:S(2)}, u32[]{:S(2)}) collective-permute-start(f32[18,8,128]{2,1,0:T(8,128)S(1)} %maximum_select_fusion), channel_id=1, source_target_pairs={{0,3},{128,129},{1,0},{129,130},{2,1},{130,131},{3,2},{131,128},{4... | collective-permute-start | bytes 221192 | tf_op jit(solution)/shard_map/ppermute | solution.py:172
  9.4 6.2 %collective-permute-start.2 = (f32[18,8,128]{2,1,0:T(8,128)S(1)}, f32[18,8,128]{2,1,0:T(8,128)S(1)}, u32[]{:S(2)}, u32[]{:S(2)}) collective-permute-start(f32[18,8,128]{2,1,0:T(8,128)S(1)} %maximum_select_fusion), channel_id=1, source_target_pairs={{0,130},{128,2},{1,131},{129,3},{2,128},{130,0},{3,129},{131,1},{4... | collective-permute-start | bytes 221192 | tf_op jit(solution)/shard_map/ppermute | solution.py:172
  15.6 12.5 %collective-permute-start.3 = (f32[4,18,8,128]{3,2,1,0:T(8,128)S(1)}, f32[4,18,8,128]{3,2,1,0:T(8,128)S(1)}, u32[]{:S(2)}, u32[]{:S(2)}) collective-permute-start(f32[4,18,8,128]{3,2,1,0:T(8,128)S(1)} %pad_maximum_fusion.2), channel_id=1, source_target_pairs={{0,16},{4,20},{8,24},{12,28},{16,32},{20,36},{24,40},{28,44},{32,4... | collective-permute-start | bytes 884744 | tf_op jit(solution)/shard_map/ppermute | solution.py:172
  16.9 11.2 %collective-permute-start.4 = (f32[4,18,8,128]{3,2,1,0:T(8,128)S(1)}, f32[4,18,8,128]{3,2,1,0:T(8,128)S(1)}, u32[]{:S(2)}, u32[]{:S(2)}) collective-permute-start(f32[4,18,8,128]{3,2,1,0:T(8,128)S(1)} %pad_maximum_fusion.2), channel_id=1, source_target_pairs={{0,32},{4,36},{8,40},{12,44},{16,48},{20,52},{24,56},{28,60},{32,0... | collective-permute-start | bytes 884744 | tf_op jit(solution)/shard_map/ppermute | solution.py:172
  17.8 10.4 %collective-permute-start.5 = (f32[4,18,8,128]{3,2,1,0:T(8,128)S(1)}, f32[4,18,8,128]{3,2,1,0:T(8,128)S(1)}, u32[]{:S(2)}, u32[]{:S(2)}) collective-permute-start(f32[4,18,8,128]{3,2,1,0:T(8,128)S(1)} %pad_maximum_fusion.2), channel_id=1, source_target_pairs={{0,48},{4,52},{8,56},{12,60},{16,0},{20,4},{24,8},{28,12},{32,16},... | collective-permute-start | bytes 884744 | tf_op jit(solution)/shard_map/ppermute | solution.py:172
  19.6 44.4 %all-to-all-start = ((f32[32,32,256]{2,1,0:T(8,128)}), f32[32,32,256]{2,1,0:T(8,128)S(1)}, u32[]{:S(2)}, u32[]{:S(2)}) async-start(f32[32,32,256]{2,1,0:T(8,128)} %select_maximum_fusion), calls=%async_computation | async-start | bytes 2097152 | tf_op jit(solution)/shard_map/all_to_all | solution.py:233
  28.5 17.2 %collective-permute-start.20 = (f32[4,4,4,8,128]{4,3,2,1,0:T(8,128)S(1)}, f32[4,4,4,8,128]{4,3,2,1,0:T(8,128)S(1)}, u32[]{:S(2)}, u32[]{:S(2)}) collective-permute-start(f32[4,4,4,8,128]{4,3,2,1,0:T(8,128)S(1)} %pad_maximum_fusion.3.refs_0_), channel_id=1, source_target_pairs={{0,4},{4,8},{8,12},{12,0},{16,20},{20,24},{24,28},{28,16},{32,36},... | collective-permute-start | bytes 786440 | tf_op jit(solution)/shard_map/ppermute | solution.py:172
  29.9 16.3 %collective-permute-start.21 = (f32[4,4,4,8,128]{4,3,2,1,0:T(8,128)S(1)}, f32[4,4,4,8,128]{4,3,2,1,0:T(8,128)S(1)}, u32[]{:S(2)}, u32[]{:S(2)}) collective-permute-start(f32[4,4,4,8,128]{4,3,2,1,0:T(8,128)S(1)} %pad_maximum_fusion.3.refs_0_), channel_id=1, source_target_pairs={{0,12},{4,0},{8,4},{12,8},{16,28},{20,16},{24,20},{28,24},{32,44},... | collective-permute-start | bytes 786440 | tf_op jit(solution)/shard_map/ppermute | solution.py:172
  31.2 28.7 %collective-permute-start.6 = (f32[2,4,14,8,128]{4,3,2,1,0:T(8,128)S(1)}, f32[2,4,14,8,128]{4,3,2,1,0:T(8,128)}, u32[]{:S(2)}, u32[]{:S(2)}) collective-permute-start(f32[2,4,14,8,128]{4,3,2,1,0:T(8,128)S(1)} %get-tuple-element.18.refs_0_), channel_id=1, source_target_pairs={{0,4},{4,8},{8,12},{12,0},{16,20},{20,24},{24,28},{28,16},{32,36},... | collective-permute-start | bytes 1376264 | tf_op jit(solution)/shard_map/ppermute | solution.py:172
  31.4 29.4 %collective-permute-start.9 = (f32[2,4,14,8,128]{4,3,2,1,0:T(8,128)S(1)}, f32[2,4,14,8,128]{4,3,2,1,0:T(8,128)}, u32[]{:S(2)}, u32[]{:S(2)}) collective-permute-start(f32[2,4,14,8,128]{4,3,2,1,0:T(8,128)S(1)} %get-tuple-element.19.refs_1_), channel_id=1, source_target_pairs={{0,12},{4,0},{8,4},{12,8},{16,28},{20,16},{24,20},{28,24},{32,44},... | collective-permute-start | bytes 1376264 | tf_op jit(solution)/shard_map/ppermute | solution.py:172
  33.9 28.9 %collective-permute-start.7 = (f32[2,4,14,8,128]{4,3,2,1,0:T(8,128)S(1)}, f32[2,4,14,8,128]{4,3,2,1,0:T(8,128)}, u32[]{:S(2)}, u32[]{:S(2)}) collective-permute-start(f32[2,4,14,8,128]{4,3,2,1,0:T(8,128)S(1)} %get-tuple-element.19.refs_1_), channel_id=1, source_target_pairs={{0,4},{4,8},{8,12},{12,0},{16,20},{20,24},{24,28},{28,16},{32,36},... | collective-permute-start | bytes 1376264 | tf_op jit(solution)/shard_map/ppermute | solution.py:172
  45.6 17.1 %collective-permute-start.8 = (f32[2,4,14,8,128]{4,3,2,1,0:T(8,128)S(1)}, f32[2,4,14,8,128]{4,3,2,1,0:T(8,128)S(1)}, u32[]{:S(2)}, u32[]{:S(2)}) collective-permute-start(f32[2,4,14,8,128]{4,3,2,1,0:T(8,128)S(1)} %get-tuple-element.18.refs_0_), channel_id=1, source_target_pairs={{0,12},{4,0},{8,4},{12,8},{16,28},{20,16},{24,20},{28,24},{32,44},... | collective-permute-start | bytes 1376264 | tf_op jit(solution)/shard_map/ppermute | solution.py:172
  46.2 12.4 %collective-permute-start.22 = (f32[4,4,4,8,128]{4,3,2,1,0:T(8,128)S(1)}, f32[4,4,4,8,128]{4,3,2,1,0:T(8,128)S(1)}, u32[]{:S(2)}, u32[]{:S(2)}) collective-permute-start(f32[4,4,4,8,128]{4,3,2,1,0:T(8,128)S(1)} %pad_maximum_fusion.3.refs_0_), channel_id=1, source_target_pairs={{0,8},{4,12},{8,0},{12,4},{16,24},{20,28},{24,16},{28,20},{32,40},... | collective-permute-start | bytes 786440 | tf_op jit(solution)/shard_map/ppermute | solution.py:172
  58.6 5.4 %collective-permute-start.13 = (f32[2,4,14,8,128]{4,3,2,1,0:T(8,128)S(1)}, f32[2,4,14,8,128]{4,3,2,1,0:T(8,128)}, u32[]{:S(2)}, u32[]{:S(2)}) collective-permute-start(f32[2,4,14,8,128]{4,3,2,1,0:T(8,128)S(1)} %get-tuple-element.19.refs_1_), channel_id=1, source_target_pairs={{0,64},{64,0},{1,65},{65,1},{2,66},{66,2},{3,67},{67,3},{4,68},{68... | collective-permute-start | bytes 1376264 | tf_op jit(solution)/shard_map/ppermute | solution.py:172
  60.0 8.9 %collective-permute-start.10 = (f32[2,4,14,8,128]{4,3,2,1,0:T(8,128)}, f32[2,4,14,8,128]{4,3,2,1,0:T(8,128)}, u32[]{:S(2)}, u32[]{:S(2)}) collective-permute-start(f32[2,4,14,8,128]{4,3,2,1,0:T(8,128)} %collective-permute-done.6.refs_2_), channel_id=1, source_target_pairs={{0,4},{4,8},{8,12},{12,0},{16,20},{20,24},{24,28},{28,16},{32,36},... | collective-permute-start | bytes 1376264 | tf_op jit(solution)/shard_map/ppermute | solution.py:172
  60.8 8.5 %collective-permute-start.11 = (f32[2,4,14,8,128]{4,3,2,1,0:T(8,128)}, f32[2,4,14,8,128]{4,3,2,1,0:T(8,128)}, u32[]{:S(2)}, u32[]{:S(2)}) collective-permute-start(f32[2,4,14,8,128]{4,3,2,1,0:T(8,128)} %collective-permute-done.9.refs_5_), channel_id=1, source_target_pairs={{0,12},{4,0},{8,4},{12,8},{16,28},{20,16},{24,20},{28,24},{32,44},... | collective-permute-start | bytes 1376264 | tf_op jit(solution)/shard_map/ppermute | solution.py:172
  62.8 7.5 %collective-permute-start.14 = (f32[2,4,14,8,128]{4,3,2,1,0:T(8,128)}, f32[2,4,14,8,128]{4,3,2,1,0:T(8,128)}, u32[]{:S(2)}, u32[]{:S(2)}) collective-permute-start(f32[2,4,14,8,128]{4,3,2,1,0:T(8,128)} %collective-permute-done.6.refs_2_), channel_id=1, source_target_pairs={{0,64},{64,0},{1,65},{65,1},{2,66},{66,2},{3,67},{67,3},{4,68},{68... | collective-permute-start | bytes 1376264 | tf_op jit(solution)/shard_map/ppermute | solution.py:172
  63.6 6.7 %collective-permute-start.15 = (f32[2,4,14,8,128]{4,3,2,1,0:T(8,128)}, f32[2,4,14,8,128]{4,3,2,1,0:T(8,128)}, u32[]{:S(2)}, u32[]{:S(2)}) collective-permute-start(f32[2,4,14,8,128]{4,3,2,1,0:T(8,128)} %collective-permute-done.7.refs_3_), channel_id=1, source_target_pairs={{0,64},{64,0},{1,65},{65,1},{2,66},{66,2},{3,67},{67,3},{4,68},{68... | collective-permute-start | bytes 1376264 | tf_op jit(solution)/shard_map/ppermute | solution.py:172
  64.1 6.7 %collective-permute-start.16 = (f32[2,4,14,8,128]{4,3,2,1,0:T(8,128)}, f32[2,4,14,8,128]{4,3,2,1,0:T(8,128)S(1)}, u32[]{:S(2)}, u32[]{:S(2)}) collective-permute-start(f32[2,4,14,8,128]{4,3,2,1,0:T(8,128)} %copy-done.5), channel_id=1, source_target_pairs={{0,64},{64,0},{1,65},{65,1},{2,66},{66,2},{3,67},{67,3},{4,68},{68... | collective-permute-start | bytes 1376264 | tf_op jit(solution)/shard_map/ppermute | solution.py:172
  70.8 15.5 %collective-permute-start.23 = (f32[4,4,4,8,128]{4,3,2,1,0:T(8,128)S(1)}, f32[4,4,4,8,128]{4,3,2,1,0:T(8,128)}, u32[]{:S(2)}, u32[]{:S(2)}) collective-permute-start(f32[4,4,4,8,128]{4,3,2,1,0:T(8,128)S(1)} %pad_maximum_fusion.3.refs_0_), channel_id=1, source_target_pairs={{0,64},{64,0},{1,65},{65,1},{2,66},{66,2},{3,67},{67,3},{4,68},{68... | collective-permute-start | bytes 786440 | tf_op jit(solution)/shard_map/ppermute | solution.py:172
  71.0 15.3 %collective-permute-start.24 = (f32[4,4,4,8,128]{4,3,2,1,0:T(8,128)S(1)}, f32[4,4,4,8,128]{4,3,2,1,0:T(8,128)}, u32[]{:S(2)}, u32[]{:S(2)}) collective-permute-start(f32[4,4,4,8,128]{4,3,2,1,0:T(8,128)S(1)} %collective-permute-done.20.refs_1_), channel_id=1, source_target_pairs={{0,64},{64,0},{1,65},{65,1},{2,66},{66,2},{3,67},{67,3},{4,68},{68... | collective-permute-start | bytes 786440 | tf_op jit(solution)/shard_map/ppermute | solution.py:172
  72.1 14.3 %collective-permute-start.25 = (f32[4,4,4,8,128]{4,3,2,1,0:T(8,128)}, f32[4,4,4,8,128]{4,3,2,1,0:T(8,128)}, u32[]{:S(2)}, u32[]{:S(2)}) collective-permute-start(f32[4,4,4,8,128]{4,3,2,1,0:T(8,128)} %copy-done.8), channel_id=1, source_target_pairs={{0,64},{64,0},{1,65},{65,1},{2,66},{66,2},{3,67},{67,3},{4,68},{68... | collective-permute-start | bytes 786440 | tf_op jit(solution)/shard_map/ppermute | solution.py:172
  72.7 13.6 %collective-permute-start.26 = (f32[4,4,4,8,128]{4,3,2,1,0:T(8,128)}, f32[4,4,4,8,128]{4,3,2,1,0:T(8,128)}, u32[]{:S(2)}, u32[]{:S(2)}) collective-permute-start(f32[4,4,4,8,128]{4,3,2,1,0:T(8,128)} %copy-done.9), channel_id=1, source_target_pairs={{0,64},{64,0},{1,65},{65,1},{2,66},{66,2},{3,67},{67,3},{4,68},{68... | collective-permute-start | bytes 786440 | tf_op jit(solution)/shard_map/ppermute | solution.py:172
  (14 other events, 228.1 us)
